TPU v7x, 32 devices: a whole 2x2x4 slice. The times are simulated.
32 devices in a mesh: segment: 2 (over core), grp: 16 (over z, y, x).
Axes of the slice: x: 2, y: 2, z: 4, core: 2. Of those that a mesh axis runs over, the one named last changes fastest.
Arguments:
- monomer_density: bfloat16 [128, 9216], P('grp'), may hold values from -3 to 3
- monomer_centers: float32 [3, 128], replicated, may hold values from 0 to 8
- dimer_pairs: int32 [2, 256], replicated, may hold values from 0 to 127, as said below
- basis_sizes: int32 [128], replicated, may hold values from 48 to 96
- dimer_core: float32 [256, 36864], P('grp')
- esp_map: float32 [96, 192], replicated, may hold values from -0.1875 to 0.1875
- repulsion: float32 [36864], replicated, may hold values from 0.005 to 0.05
Outputs:
- section_out: float32 [2, 256, 36864], P('segment', 'grp')
- window_energy: float32 [], replicated
Inputs may be any that keep to these rules, and one draw needn't show every extreme that they name: `dimer_pairs`: the two monomers of a dimer differ.
All inputs are finite; a program needn't handle non-finite values. Where the computation divides by a largest or mean magnitude, that divisor is 1e-20 or more.
Results may differ from a plain program's by a relative error of at most 0.00045.
Values may be sent and summed in bfloat16 or wider, within the bound.
A program may use at most 128 MiB of HBM per device.

v0:
```python
import functools

import jax
import jax.numpy as jnp
from jax import lax
from jax.experimental import pallas as pl
from jax.experimental.pallas import tpu as pltpu
from jax.sharding import PartitionSpec as P

PURIFY = 8
epsilon = 1e-06
LANES = 128
MESH = pl.DeviceIdType.MESH
FIRST_PLAN = ((1, 1),) * PURIFY
LAST_PLAN = ((1, 1),) * (PURIFY - 3) + ((3, 3),) * 3


def flow_orders(groups):
    top, *rest = reversed([1 << k for k in range(groups.bit_length() - 1)])
    return [[top] + rest[f * len(rest) // 3:] + rest[:f * len(rest) // 3] for f in range(3)]


def bf(value):
    return value.astype(jnp.bfloat16)


def dot(left, right):
    return jnp.dot(left, right, preferred_element_type=jnp.float32)


def split(value):
    high = bf(value)
    return high, bf(value - high.astype(jnp.float32))


def product(left, right, passes):
    if passes == 1:
        return dot(bf(left), bf(right))
    left_high, left_low = split(left)
    right_high, right_low = split(right)
    return dot(left_high, right_high) + (dot(left_high, right_low) + dot(left_low, right_high))


def iota(shape, axis):
    return lax.broadcasted_iota(jnp.int32, shape, axis)


def pair_ids(pairs_ref, positions):
    count = positions.shape[0]
    hit = iota((count, pairs_ref.shape[1]), 1) == positions
    out = []
    for side in range(2):
        row = pairs_ref[side:side + 1, :].astype(jnp.float32)
        out.append(jnp.sum(jnp.where(hit, row, 0.0), axis=1, keepdims=True).astype(jnp.int32))
    return out


def field_kernel(groups, density_ref, centers_ref, pairs_ref, field_ref, blocks, staged, send_sem, recv_sem, own_sem, part_send, part_recv, out_sem):
    me = lax.axis_index("grp")
    seg = lax.axis_index("segment")
    rows, total = density_ref.shape
    orders = flow_orders(groups)
    flows = len(orders)
    stages = len(orders[0])
    half = total // 2
    width = half // flows
    tiles = half // LANES
    monomers = centers_ref.shape[1]
    dims = pairs_ref.shape[1] // groups
    mine = dims // 2

    barrier = pltpu.get_barrier_semaphore()
    for bit in sorted(orders[0]):
        pl.semaphore_signal(barrier, inc=1, device_id=(seg, me ^ bit), device_id_type=MESH)
    pl.semaphore_signal(barrier, inc=1, device_id=(1 - seg, me), device_id_type=MESH)

    own = []
    for f in range(flows):
        start = pl.multiple_of(seg * half + f * width, LANES)
        source = density_ref.at[:, pl.ds(start, width)]
        copy = pltpu.make_async_copy(source, blocks.at[f, 0], own_sem.at[f])
        copy.start()
        own.append(copy)
    pl.semaphore_wait(barrier, stages + 1)

    def exchange(f, k):
        count = 1 << k
        return pltpu.make_async_remote_copy(
            src_ref=blocks.at[f, pl.ds(0, count)],
            dst_ref=blocks.at[f, pl.ds(count, count)],
            send_sem=send_sem.at[f, k],
            recv_sem=recv_sem.at[f, k],
            device_id=(seg, me ^ orders[f][k]),
            device_id_type=MESH,
        )

    for f in range(flows):
        own[f].wait()
        exchange(f, 0).start()

    place = iota((dims, 1), 0)
    is_own = place < mine
    positions = me * dims + jnp.where(is_own, seg * mine + place, (1 - seg) * mine + place - mine)
    first_ids, second_ids = pair_ids(pairs_ref, positions)
    labels = iota((dims, monomers), 1)
    is_first = labels == first_ids
    is_second = labels == second_ids
    distance = jnp.zeros((dims, monomers), jnp.float32)
    for axis in range(centers_ref.shape[0]):
        row = centers_ref[axis:axis + 1, :]
        first_at = jnp.sum(jnp.where(is_first, row, 0.0), axis=1, keepdims=True)
        second_at = jnp.sum(jnp.where(is_second, row, 0.0), axis=1, keepdims=True)
        gap = 0.5 * (first_at + second_at) - row
        distance = distance + gap * gap
    weights = jnp.where(is_first | is_second, 0.0, 1.0 / jnp.sqrt(distance + 1.0))
    weights = bf(weights)
    ordered = []
    for f in range(flows):
        column = iota((monomers, monomers), 1)
        slot = column // rows
        owner = jnp.full_like(column, me)
        for k, bit in enumerate(orders[f]):
            owner = owner ^ jnp.where((slot & (1 << k)) != 0, bit, 0)
        label = owner * rows + (column & (rows - 1))
        chosen = bf(jnp.where(iota((monomers, monomers), 0) == label, 1.0, 0.0))
        ordered.append(bf(dot(weights, chosen)))

    for k in range(1, stages):
        for f in range(flows):
            exchange(f, k - 1).wait()
            exchange(f, k).start()

    for f in range(flows):
        exchange(f, stages - 1).wait()
        gathered = bf(blocks[f].astype(jnp.float32).reshape(monomers, width))
        result = dot(ordered[f], gathered)
        for t in range(width // LANES):
            piece = result[:, t * LANES:(t + 1) * LANES]
            staged[0, f * (width // LANES) + t] = piece[:mine]
            staged[1, f * (width // LANES) + t] = piece[mine:]

    target = field_ref.at[pl.ds(seg * tiles, tiles)]
    give = pltpu.make_async_remote_copy(
        src_ref=staged.at[1], dst_ref=target, send_sem=part_send, recv_sem=part_recv,
        device_id=(1 - seg, me), device_id_type=MESH,
    )
    give.start()
    keep = pltpu.make_async_copy(staged.at[0], target, out_sem)
    keep.start()
    keep.wait()
    give.wait()


def make_field(groups, density, centers, pairs):
    rows, total = density.shape
    flows = len(flow_orders(groups))
    stages = groups.bit_length() - 1
    half = total // 2
    mine = pairs.shape[1] // groups // 2
    vmem = pl.BlockSpec(memory_space=pltpu.VMEM)
    return pl.pallas_call(
        functools.partial(field_kernel, groups),
        out_shape=jax.ShapeDtypeStruct((total // LANES, mine, LANES), jnp.float32),
        in_specs=[pl.BlockSpec(memory_space=pl.ANY), vmem, vmem],
        out_specs=vmem,
        scratch_shapes=[
            pltpu.VMEM((flows, groups, rows, half // flows), jnp.bfloat16),
            pltpu.VMEM((2, half // LANES, mine, LANES), jnp.float32),
            pltpu.SemaphoreType.DMA((flows, stages)),
            pltpu.SemaphoreType.DMA((flows, stages)),
            pltpu.SemaphoreType.DMA((flows,)),
            pltpu.SemaphoreType.DMA,
            pltpu.SemaphoreType.DMA,
            pltpu.SemaphoreType.DMA,
        ],
        compiler_params=pltpu.CompilerParams(collective_id=0, has_side_effects=True),
    )(density, centers, pairs)


def rolled(value, shift):
    return pltpu.roll(value, shift, 1)


def load_field(field_ref, buffer, d, mine, width):
    count = width * width // LANES // 3
    a, b, c = [field_ref[pl.ds(j * mine + d, count, stride=3 * mine), :] for j in range(3)]
    lane = iota((count, LANES), 1)
    buffer[pl.ds(0, count, stride=4), :] = a
    buffer[pl.ds(1, count, stride=4), :] = jnp.where(lane < 32, rolled(a, 32), rolled(b, 32))
    buffer[pl.ds(2, count, stride=4), :] = jnp.where(lane < 64, rolled(b, 64), rolled(c, 64))
    buffer[pl.ds(3, count, stride=4), :] = rolled(c, 96)
    return buffer[:, :width]


def load_square(source, low, high, d, mine, full):
    count = full // 2
    a, b, c = [source[pl.ds(j * mine + d, count, stride=3 * mine), :] for j in range(3)]
    lane = iota((count, LANES), 1)
    shifted = rolled(c, 64)
    low[pl.ds(0, count, stride=2), :] = a
    high[pl.ds(0, count, stride=2), :] = b
    low[pl.ds(1, count, stride=2), :] = jnp.where(lane < 64, rolled(b, 64), shifted)
    high[pl.ds(1, count, stride=2), :] = shifted
    return jnp.concatenate([low[...], high[:, :full - LANES]], axis=1)


def store_square(target, value, low, high, d, mine, full):
    count = full // 2
    low[...] = value[:, :LANES]
    high[:, :full - LANES] = value[:, LANES:]
    lane = iota((count, LANES), 1)
    even_low = low[pl.ds(0, count, stride=2), :]
    even_high = high[pl.ds(0, count, stride=2), :]
    odd_low = rolled(low[pl.ds(1, count, stride=2), :], 64)
    odd_high = rolled(high[pl.ds(1, count, stride=2), :], 64)
    pieces = (even_low, jnp.where(lane < 64, even_high, odd_low), jnp.where(lane < 64, odd_low, odd_high))
    for j, piece in enumerate(pieces):
        target[pl.ds(j * mine + d, count, stride=3 * mine), :] = piece


def solve_kernel(groups, field_ref, sizes_ref, pairs_ref, core_ref, map_ref, rep_ref, section_ref, energy_ref, core_buf, low, high, fbuf, fock, iterate, core_sem):
    me = lax.axis_index("grp")
    seg = lax.axis_index("segment")
    width, full = map_ref.shape
    dims = pairs_ref.shape[1] // groups
    mine = dims // 2
    fetch = pltpu.make_async_copy(core_ref.at[seg], core_buf, core_sem)
    fetch.start()

    positions = me * dims + seg * mine + iota((mine, 1), 0)
    ids = pair_ids(pairs_ref, positions)
    labels = iota((mine, sizes_ref.shape[1]), 1)
    sizes = [
        jnp.sum(jnp.where(labels == i, sizes_ref[...].astype(jnp.float32), 0.0), axis=1, keepdims=True)
        for i in ids
    ]
    row_at = iota((1, full), 1)
    column_at = iota((full, 1), 0)
    eye = iota((full, full), 0) == iota((full, full), 1)
    rep_low, rep_high = low.at[0], high.at[0]
    repulsion = load_square(rep_ref, rep_low, rep_high, 0, 1, full)
    symmetric = 0.5 * (repulsion + repulsion.T)
    mapping = map_ref[...]
    mapping_t = mapping.T

    def live(d):
        first, second = [s[d:d + 1, :] for s in sizes]
        out = []
        for at in (row_at, column_at):
            limit = jnp.where(at < width, first, second + width)
            out.append(jnp.where(at.astype(jnp.float32) < limit, 1.0, 0.0))
        return out, first + second

    def total(value):
        return jnp.sum(jnp.sum(value, axis=0, keepdims=True), axis=1, keepdims=True)

    def begin(matrix, d):
        (live_row, live_column), count = live(d)
        masked = matrix * (live_column * live_row)
        chemical = total(jnp.where(eye, masked, 0.0)) / count
        shifted = masked - jnp.where(eye, chemical * live_row, 0.0)
        radius = jnp.max(jnp.sum(jnp.abs(shifted), axis=0, keepdims=True), axis=1, keepdims=True)
        iterate[d] = shifted * (-1.0 / (radius + epsilon))

    def step(passes):
        first, second = passes
        values = [iterate[d] for d in range(mine)]
        squares = [product(x, x, first) for x in values]
        for d in range(mine):
            x = values[d]
            iterate[d] = 1.5 * x - 0.5 * product(x, squares[d], second)

    def run(plan):
        at = 0
        while at < len(plan):
            length = 1
            while at + length < len(plan) and plan[at + length] == plan[at]:
                length += 1
            passes = plan[at]

            def body(i, carry):
                step(passes)
                return carry

            lax.fori_loop(0, length, body, 0)
            at += length

    def finish(d):
        (live_row, live_column), count = live(d)
        return 0.5 * (iterate[d] + jnp.where(eye, live_row, 0.0)), count

    fetch.wait()
    for d in range(mine):
        field = load_field(field_ref, fbuf.at[d], d, mine, width)
        potential = product(mapping_t, product(field, mapping, 3), 3)
        value = load_square(core_buf, low.at[d], high.at[d], d, mine, full) + potential
        value = 0.5 * (value + value.T)
        fock[d] = value
        begin(value, d)
    for d in range(mine):
        store_square(section_ref.at[0], fock[d], low.at[d], high.at[d], d, mine, full)
    run(FIRST_PLAN)
    for d in range(mine):
        density, count = finish(d)
        occupied = jnp.sum(jnp.where(eye, density, 0.0), axis=1, keepdims=True)
        coulomb = jnp.sum(symmetric * occupied, axis=0, keepdims=True)
        change = jnp.where(eye, coulomb, 0.0) - 0.5 * symmetric * density
        core_fock = fock[d]
        begin(core_fock + change, d)
        fock[d] = 2.0 * core_fock + change
    run(LAST_PLAN)
    energy = jnp.zeros((1, 1), jnp.float32)
    for d in range(mine):
        density, count = finish(d)
        energy = energy + 0.5 * total(density * fock[d]) / count
        store_square(section_ref.at[1], density, low.at[d], high.at[d], d, mine, full)
    energy_ref[...] = jnp.broadcast_to(energy, energy_ref.shape)


def solve(groups, field, sizes, pairs, core, mapping, repulsion):
    width, full = mapping.shape
    mine = pairs.shape[1] // groups // 2
    tiles = full * full // LANES
    vmem = pl.BlockSpec(memory_space=pltpu.VMEM)
    return pl.pallas_call(
        functools.partial(solve_kernel, groups),
        out_shape=(
            jax.ShapeDtypeStruct((2, tiles * mine, LANES), jnp.float32),
            jax.ShapeDtypeStruct((8, LANES), jnp.float32),
        ),
        in_specs=[vmem, vmem, vmem, pl.BlockSpec(memory_space=pl.ANY), vmem, vmem],
        out_specs=(vmem, vmem),
        scratch_shapes=[
            pltpu.VMEM((tiles * mine, LANES), jnp.float32),
            pltpu.VMEM((mine, full, LANES), jnp.float32),
            pltpu.VMEM((mine, full, LANES), jnp.float32),
            pltpu.VMEM((mine, width, LANES), jnp.float32),
            pltpu.VMEM((mine, full, full), jnp.float32),
            pltpu.VMEM((mine, full, full), jnp.float32),
            pltpu.SemaphoreType.DMA,
        ],
    )(field, sizes, pairs, core, mapping, repulsion)


def share_kernel(groups, energy_ref, section_ref, total_ref, out_ref, gathered, send_sem, recv_sem, part_send, part_recv, own_sem):
    me = lax.axis_index("grp")
    seg = lax.axis_index("segment")
    count = 2 * groups
    index = seg * groups + me
    barrier = pltpu.get_barrier_semaphore()

    def place(offset):
        other = lax.rem(index + offset, count)
        return other // groups, lax.rem(other, groups)

    for offset in range(1, count):
        pl.semaphore_signal(barrier, inc=1, device_id=place(offset), device_id_type=MESH)
    keep = pltpu.make_async_copy(section_ref.at[seg], out_ref.at[seg], own_sem)
    keep.start()
    pl.semaphore_wait(barrier, count - 1)
    give = pltpu.make_async_remote_copy(
        src_ref=section_ref.at[1 - seg], dst_ref=out_ref.at[seg], send_sem=part_send, recv_sem=part_recv,
        device_id=(1 - seg, me), device_id_type=MESH,
    )
    give.start()
    copies = []
    for offset in range(1, count):
        copy = pltpu.make_async_remote_copy(
            src_ref=energy_ref, dst_ref=gathered.at[index], send_sem=send_sem.at[offset], recv_sem=recv_sem.at[offset],
            device_id=place(offset), device_id_type=MESH,
        )
        copy.start()
        copies.append(copy)
    gathered[index] = energy_ref[...]
    for copy in copies:
        copy.wait()
    total_ref[...] = jnp.sum(gathered[...], axis=0)
    keep.wait()
    give.wait()


def share(groups, energy, section):
    count = 2 * groups
    anywhere = pl.BlockSpec(memory_space=pl.ANY)
    vmem = pl.BlockSpec(memory_space=pltpu.VMEM)
    return pl.pallas_call(
        functools.partial(share_kernel, groups),
        out_shape=(
            jax.ShapeDtypeStruct(energy.shape, jnp.float32),
            jax.ShapeDtypeStruct(section.shape, jnp.float32),
        ),
        in_specs=[vmem, vmem],
        out_specs=(vmem, vmem),
        scratch_shapes=[
            pltpu.VMEM((count,) + energy.shape, jnp.float32),
            pltpu.SemaphoreType.DMA((count,)),
            pltpu.SemaphoreType.DMA((count,)),
            pltpu.SemaphoreType.DMA,
            pltpu.SemaphoreType.DMA,
            pltpu.SemaphoreType.DMA,
        ],
        compiler_params=pltpu.CompilerParams(collective_id=1, has_side_effects=True),
    )(energy, section)


def on_device(groups, monomer_density, monomer_centers, dimer_pairs, basis_sizes, dimer_core, esp_map, repulsion):
    dims, flat = dimer_core.shape
    mine = dims // 2
    tiles = flat // LANES
    core = dimer_core.reshape(2, mine, tiles, LANES).transpose(0, 2, 1, 3).reshape(2, tiles * mine, LANES)
    field = make_field(groups, monomer_density, monomer_centers, dimer_pairs)
    field = field.reshape(-1, LANES)
    section, energy = solve(
        groups, field, basis_sizes.reshape(1, -1), dimer_pairs, core, esp_map, repulsion.reshape(tiles, LANES)
    )
    total, section = share(groups, energy, section)
    section = section.reshape(2, tiles, mine, LANES).transpose(0, 2, 1, 3).reshape(1, dims, flat)
    return section, total[0, 0] / dimer_pairs.shape[1]


def solution(mesh):
    in_specs = (P("grp", None), P(), P(), P(), P("grp", None), P(), P())
    out_specs = (P("segment", "grp", None), P())
    return jax.shard_map(
        functools.partial(on_device, mesh.shape["grp"]), mesh=mesh, in_specs=in_specs, out_specs=out_specs, check_vma=False
    )
```

profile of v0, /device:TPU:0, one launch (start us, length us, event | category | flops | bytes accessed | tf_op | source)
XLA Modules:
  0.0 64.3 jit_solution(3168489391647322662)
XLA Ops:
  0.6 25.2 %shard_map.86 = f32[72,8,128]{2,1,0:T(8,128)} custom-call(bf16[8,9216]{1,0:T(8,128)(2,1)} %density_ref.1, f32[3,128]{1,0:T(4,128)} %centers_ref.1, s32[2,256]{1,0:T(2,128)} %pairs_ref.3), custom_call_target="tpu_custom_call" | custom-call | tf_op jit(solution)/shard_map/pallas_call | solution.py:161
  25.9 19.7 %shard_map.87 = (f32[2,2304,128]{2,1,0:T(8,128)}, f32[8,128]{1,0:T(8,128)}) custom-call(f32[576,128]{1,0:T(8,128)} %bitcast.16, s32[1,128]{1,0:T(1,128)} %bitcast.18, s32[2,256]{1,0:T(2,128)} %pairs_ref.3, f32[2,2304,128]{2,1,0:T(8,128)} %bitcast.14, f32[96,192]{1,0:T(8,128)} %map_ref.1, f32[288,128]{1,0:T(8,128)} %bitcast.17), custom_call_target="tpu_custom_call" | custom-call | tf_op jit(solution)/shard_map/pallas_call | solution.py:325
  45.6 12.5 %shard_map.88 = (f32[8,128]{1,0:T(8,128)}, f32[2,2304,128]{2,1,0:T(8,128)}) custom-call(f32[8,128]{1,0:T(8,128)} %get-tuple-element.6.energy_ref, f32[2,2304,128]{2,1,0:T(8,128)} %get-tuple-element.7.section_ref), custom_call_target="tpu_custom_call" | custom-call | tf_op jit(solution)/shard_map/pallas_call | solution.py:386
  58.1 1.2 %slice.3 = f32[1,1]{1,0:T(1,128)} slice(f32[8,128]{1,0:T(8,128)} %get-tuple-element.9), slice={[0:1], [0:1]} | slice | bytes 8 | tf_op jit(solution)/shard_map/slice | solution.py:418
  59.9 3.2 %copy.10 = f32[1,16,36864]{2,1,0:T(8,128)} copy(f32[1,16,36864]{2,1,0:T(8,128)} %bitcast.15) | data formatting | bytes 4718592
where the time goes:
time: 64.6 us; the launch traced here: 64.3 us
  Pallas kernels  57.5 us (89%)
  local copies, waits for them, and re-layouts  4.4 us (7%)
  between operations  2.44 us (4%)
    pallas_call x1, Pallas kernels, make_field(): pl.pallas_call(functools.partial(field_kernel, groups), out_shape=jax.Sha...  25.2 us
    pallas_call x1, Pallas kernels, solve(): pl.pallas_call(functools.partial(solve_kernel, groups), out_shape=(jax.Sh...  19.7 us
    pallas_call x1, Pallas kernels, share(): pl.pallas_call(functools.partial(share_kernel, groups), out_shape=(jax.Sh...  12.5 us
    unnamed x1, local copies, waits for them, and re-layouts  3.22 us

commit v1 on v0

v1 whole, which is shorter than its diff:
```python
import functools

import jax
import jax.numpy as jnp
from jax import lax
from jax.experimental import pallas as pl
from jax.experimental.pallas import tpu as pltpu
from jax.sharding import PartitionSpec as P

PURIFY = 8
epsilon = 1e-06
LANES = 128
SPLITS = 2
KEEP = pltpu.VMEM
MESH = pl.DeviceIdType.MESH
FIRST_PLAN = ((1, 1),) * PURIFY
LAST_PLAN = ((1, 1),) * (PURIFY - 3) + ((3, 3),) * 3


def flow_orders(groups):
    top, *rest = reversed([1 << k for k in range(groups.bit_length() - 1)])
    orders = [[top] + rest[f * len(rest) // 3:] + rest[:f * len(rest) // 3] for f in range(3)]
    return orders * SPLITS


def bf(value):
    return value.astype(jnp.bfloat16)


def dot(left, right):
    return jnp.dot(left, right, preferred_element_type=jnp.float32)


def split(value):
    high = bf(value)
    return high, bf(value - high.astype(jnp.float32))


def product(left, right, passes):
    if passes == 1:
        return dot(bf(left), bf(right))
    left_high, left_low = split(left)
    right_high, right_low = split(right)
    return dot(left_high, right_high) + (dot(left_high, right_low) + dot(left_low, right_high))


def iota(shape, axis):
    return lax.broadcasted_iota(jnp.int32, shape, axis)


def pair_ids(pairs_ref, positions):
    count = positions.shape[0]
    hit = iota((count, pairs_ref.shape[1]), 1) == positions
    out = []
    for side in range(2):
        row = pairs_ref[side:side + 1, :].astype(jnp.float32)
        out.append(jnp.sum(jnp.where(hit, row, 0.0), axis=1, keepdims=True).astype(jnp.int32))
    return out


def rolled(value, shift):
    return pltpu.roll(value, shift, 1)


def load_field(field_ref, buffer, d, width):
    count = width * width // LANES // 3
    a, b, c = [field_ref[pl.ds(j, count, stride=3), d, :] for j in range(3)]
    lane = iota((count, LANES), 1)
    buffer[pl.ds(0, count, stride=4), :] = a
    buffer[pl.ds(1, count, stride=4), :] = jnp.where(lane < 32, rolled(a, 32), rolled(b, 32))
    buffer[pl.ds(2, count, stride=4), :] = jnp.where(lane < 64, rolled(b, 64), rolled(c, 64))
    buffer[pl.ds(3, count, stride=4), :] = rolled(c, 96)
    return buffer[:, :width]


def load_square(source, low, high, d, mine, full):
    count = full // 2
    a, b, c = [source[pl.ds(j * mine + d, count, stride=3 * mine), :] for j in range(3)]
    lane = iota((count, LANES), 1)
    shifted = rolled(c, 64)
    low[pl.ds(0, count, stride=2), :] = a
    high[pl.ds(0, count, stride=2), :] = b
    low[pl.ds(1, count, stride=2), :] = jnp.where(lane < 64, rolled(b, 64), shifted)
    high[pl.ds(1, count, stride=2), :] = shifted
    return jnp.concatenate([low[...], high[:, :full - LANES]], axis=1)


def store_square(target, value, low, high, full):
    count = full // 2
    low[...] = value[:, :LANES]
    high[:, :full - LANES] = value[:, LANES:]
    lane = iota((count, LANES), 1)
    even_low = low[pl.ds(0, count, stride=2), :]
    even_high = high[pl.ds(0, count, stride=2), :]
    odd_low = rolled(low[pl.ds(1, count, stride=2), :], 64)
    odd_high = rolled(high[pl.ds(1, count, stride=2), :], 64)
    pieces = (even_low, jnp.where(lane < 64, even_high, odd_low), jnp.where(lane < 64, odd_low, odd_high))
    for j, piece in enumerate(pieces):
        target[pl.ds(j, count, stride=3), :] = piece


def solve_kernel(
    groups, density_ref, centers_ref, pairs_ref, sizes_ref, core_ref, map_ref, rep_ref,
    stage_ref, arrived_ref, gathered,
    blocks, given, field_ref, core_buf, low, high, fbuf, fock, iterate, energy_ref,
    send_sem, recv_sem, own_sem, part_send, part_recv, sum_send, sum_recv, section_send, section_recv, core_sem,
):
    me = lax.axis_index("grp")
    seg = lax.axis_index("segment")
    rows, flat = density_ref.shape
    orders = flow_orders(groups)
    flows = len(orders)
    stages = len(orders[0])
    half = flat // 2
    columns = half // flows
    tiles = half // LANES
    each = columns // LANES
    monomers = centers_ref.shape[1]
    width, full = map_ref.shape
    dims = pairs_ref.shape[1] // groups
    mine = dims // 2
    devices = 2 * groups
    index = seg * groups + me

    def place_of(offset):
        other = lax.rem(index + offset, devices)
        return other // groups, lax.rem(other, groups)

    barrier = pltpu.get_barrier_semaphore()
    for offset in range(1, devices):
        pl.semaphore_signal(barrier, inc=1, device_id=place_of(offset), device_id_type=MESH)
    own = []
    for f in range(flows):
        start = pl.multiple_of(seg * half + f * columns, LANES)
        source = density_ref.at[:, pl.ds(start, columns)]
        copy = pltpu.make_async_copy(source, blocks.at[f, 0], own_sem.at[f])
        copy.start()
        own.append(copy)
    fetch = pltpu.make_async_copy(core_ref.at[seg], core_buf, core_sem)
    fetch.start()
    pl.semaphore_wait(barrier, devices - 1)

    def exchange(f, k):
        count = 1 << k
        return pltpu.make_async_remote_copy(
            src_ref=blocks.at[f, pl.ds(0, count)],
            dst_ref=blocks.at[f, pl.ds(count, count)],
            send_sem=send_sem.at[f, k],
            recv_sem=recv_sem.at[f, k],
            device_id=(seg, me ^ orders[f][k]),
            device_id_type=MESH,
        )

    for f in range(flows):
        own[f].wait()
        exchange(f, 0).start()

    place = iota((dims, 1), 0)
    positions = me * dims + jnp.where(place < mine, seg * mine + place, (1 - seg) * mine + place - mine)
    ids = pair_ids(pairs_ref, positions)
    labels = iota((dims, monomers), 1)
    is_first, is_second = [labels == i for i in ids]
    distance = jnp.zeros((dims, monomers), jnp.float32)
    for axis in range(centers_ref.shape[0]):
        row = centers_ref[axis:axis + 1, :]
        first_at = jnp.sum(jnp.where(is_first, row, 0.0), axis=1, keepdims=True)
        second_at = jnp.sum(jnp.where(is_second, row, 0.0), axis=1, keepdims=True)
        gap = 0.5 * (first_at + second_at) - row
        distance = distance + gap * gap
    weights = bf(jnp.where(is_first | is_second, 0.0, 1.0 / jnp.sqrt(distance + 1.0)))
    ordered = []
    for f in range(flows // SPLITS):
        column = iota((monomers, monomers), 1)
        slot = column // rows
        owner = jnp.full_like(column, me)
        for k, bit in enumerate(orders[f]):
            owner = owner ^ jnp.where((slot & (1 << k)) != 0, bit, 0)
        label = owner * rows + (column & (rows - 1))
        chosen = bf(jnp.where(iota((monomers, monomers), 0) == label, 1.0, 0.0))
        ordered.append(bf(dot(weights, chosen)))
    sizes = [
        jnp.sum(jnp.where(hit, sizes_ref[...].astype(jnp.float32), 0.0), axis=1, keepdims=True)[:mine]
        for hit in (is_first, is_second)
    ]

    for k in range(1, stages):
        for f in range(flows):
            exchange(f, k - 1).wait_recv()
            exchange(f, k).start()

    row_at = iota((1, full), 1)
    column_at = iota((full, 1), 0)
    eye = iota((full, full), 0) == iota((full, full), 1)
    repulsion = load_square(rep_ref, low.at[0], high.at[0], 0, 1, full)
    symmetric = 0.5 * (repulsion + repulsion.T)
    mapping = map_ref[...]
    mapping_t = mapping.T
    fetch.wait()
    for d in range(mine):
        value = load_square(core_buf, low.at[d], high.at[d], d, mine, full)
        fock[d] = 0.5 * (value + value.T)

    def partial(f, first, count):
        block = bf(blocks[f, first:first + count].astype(jnp.float32).reshape(count * rows, columns))
        return dot(ordered[f % (flows // SPLITS)][:, first * rows:(first + count) * rows], block)

    early = [partial(f, 0, groups // 2) for f in range(flows)]

    def give(f):
        return pltpu.make_async_remote_copy(
            src_ref=given.at[pl.ds(f * each, each)],
            dst_ref=field_ref.at[pl.ds(seg * tiles + f * each, each)],
            send_sem=part_send.at[f], recv_sem=part_recv.at[f],
            device_id=(1 - seg, me), device_id_type=MESH,
        )

    for f in range(flows):
        exchange(f, stages - 1).wait_recv()
        result = early[f] + partial(f, groups // 2, groups // 2)
        for t in range(each):
            piece = result[:, t * LANES:(t + 1) * LANES]
            field_ref[seg * tiles + f * each + t] = piece[:mine]
            given[f * each + t] = piece[mine:]
        give(f).start()
    for f in range(flows):
        for k in range(stages):
            exchange(f, k).wait_send()
    for f in range(flows):
        give(f).wait()

    def live(d):
        first, second = [s[d:d + 1, :] for s in sizes]
        out = []
        for at in (row_at, column_at):
            limit = jnp.where(at < width, first, second + width)
            out.append(jnp.where(at.astype(jnp.float32) < limit, 1.0, 0.0))
        return out, first + second

    def total(value):
        return jnp.sum(jnp.sum(value, axis=0, keepdims=True), axis=1, keepdims=True)

    def begin(matrix, d):
        (live_row, live_column), count = live(d)
        masked = matrix * (live_column * live_row)
        chemical = total(jnp.where(eye, masked, 0.0)) / count
        shifted = masked - jnp.where(eye, chemical * live_row, 0.0)
        radius = jnp.max(jnp.sum(jnp.abs(shifted), axis=0, keepdims=True), axis=1, keepdims=True)
        iterate[d] = shifted * (-1.0 / (radius + epsilon))

    def step(passes):
        first, second = passes
        values = [iterate[d] for d in range(mine)]
        squares = [product(x, x, first) for x in values]
        for d in range(mine):
            x = values[d]
            iterate[d] = 1.5 * x - 0.5 * product(x, squares[d], second)

    def run(plan):
        at = 0
        while at < len(plan):
            length = 1
            while at + length < len(plan) and plan[at + length] == plan[at]:
                length += 1
            passes = plan[at]

            def body(i, carry):
                step(passes)
                return carry

            lax.fori_loop(0, length, body, 0)
            at += length

    def finish(d):
        (live_row, live_column), count = live(d)
        return 0.5 * (iterate[d] + jnp.where(eye, live_row, 0.0)), count

    def swap(part, d):
        return pltpu.make_async_remote_copy(
            src_ref=stage_ref.at[part, d], dst_ref=arrived_ref.at[d],
            send_sem=section_send.at[d], recv_sem=section_recv.at[d],
            device_id=(1 - seg, me), device_id_type=MESH,
        )

    for d in range(mine):
        field = load_field(field_ref, fbuf.at[d], d, width)
        field = 0.5 * (field + field.T)
        value = fock[d] + product(mapping_t, product(field, mapping, 3), 3)
        fock[d] = value
        begin(value, d)
    for d in range(mine):
        store_square(stage_ref.at[0, d], fock[d], low.at[d], high.at[d], full)

    @pl.when(seg == 1)
    def _():
        for d in range(mine):
            swap(0, d).start()

    run(FIRST_PLAN)
    for d in range(mine):
        density, count = finish(d)
        occupied = jnp.sum(jnp.where(eye, density, 0.0), axis=1, keepdims=True)
        coulomb = jnp.sum(symmetric * occupied, axis=0, keepdims=True)
        change = jnp.where(eye, coulomb, 0.0) - 0.5 * symmetric * density
        core_fock = fock[d]
        begin(core_fock + change, d)
        fock[d] = 2.0 * core_fock + change
    run(LAST_PLAN)
    energy = jnp.zeros((1, 1), jnp.float32)
    for d in range(mine):
        density, count = finish(d)
        energy = energy + 0.5 * total(density * fock[d]) / count
        store_square(stage_ref.at[1, d], density, low.at[d], high.at[d], full)

        @pl.when(seg == 0)
        def _():
            swap(1, d).start()

    energy_ref[...] = jnp.broadcast_to(energy, energy_ref.shape)
    gathered[index] = energy_ref[...]
    copies = []
    for offset in range(1, devices):
        copy = pltpu.make_async_remote_copy(
            src_ref=energy_ref, dst_ref=gathered.at[index], send_sem=sum_send.at[offset], recv_sem=sum_recv.at[offset],
            device_id=place_of(offset), device_id_type=MESH,
        )
        copy.start()
        copies.append(copy)
    for copy in copies:
        copy.wait()
    for d in range(mine):
        swap(1 - seg, d).wait()


def solve(groups, density, centers, pairs, sizes, core, mapping, repulsion):
    rows, total = density.shape
    flows = len(flow_orders(groups))
    stages = groups.bit_length() - 1
    half = total // 2
    devices = 2 * groups
    width, full = mapping.shape
    mine = pairs.shape[1] // groups // 2
    tiles = full * full // LANES
    vmem = pl.BlockSpec(memory_space=pltpu.VMEM)
    anywhere = pl.BlockSpec(memory_space=pl.ANY)
    return pl.pallas_call(
        functools.partial(solve_kernel, groups),
        out_shape=(
            KEEP((2, mine, tiles, LANES), jnp.float32),
            KEEP((mine, tiles, LANES), jnp.float32),
            KEEP((devices, 1, LANES), jnp.float32),
        ),
        in_specs=[anywhere, vmem, vmem, vmem, anywhere, vmem, vmem],
        out_specs=(vmem, vmem, vmem),
        scratch_shapes=[
            pltpu.VMEM((flows, groups, rows, half // flows), jnp.bfloat16),
            pltpu.VMEM((half // LANES, mine, LANES), jnp.float32),
            pltpu.VMEM((total // LANES, mine, LANES), jnp.float32),
            pltpu.VMEM((tiles * mine, LANES), jnp.float32),
            pltpu.VMEM((mine, full, LANES), jnp.float32),
            pltpu.VMEM((mine, full, LANES), jnp.float32),
            pltpu.VMEM((mine, width, LANES), jnp.float32),
            pltpu.VMEM((mine, full, full), jnp.float32),
            pltpu.VMEM((mine, full, full), jnp.float32),
            pltpu.VMEM((1, LANES), jnp.float32),
            pltpu.SemaphoreType.DMA((flows, stages)),
            pltpu.SemaphoreType.DMA((flows, stages)),
            pltpu.SemaphoreType.DMA((flows,)),
            pltpu.SemaphoreType.DMA((flows,)),
            pltpu.SemaphoreType.DMA((flows,)),
            pltpu.SemaphoreType.DMA((devices,)),
            pltpu.SemaphoreType.DMA((devices,)),
            pltpu.SemaphoreType.DMA((mine,)),
            pltpu.SemaphoreType.DMA((mine,)),
            pltpu.SemaphoreType.DMA,
        ],
        compiler_params=pltpu.CompilerParams(collective_id=0, has_side_effects=True, vmem_limit_bytes=40 << 20),
    )(density, centers, pairs, sizes, core, mapping, repulsion)


def merge_kernel(share, stage_ref, arrived_ref, gathered, out_ref, total_ref):
    seg = lax.axis_index("segment")
    half = pl.program_id(0)
    mine, tiles, _ = arrived_ref.shape

    @pl.when(half == 0)
    def _():
        total_ref[...] = jnp.sum(gathered[...], axis=0)[:, :1] * share

    @pl.when(half == seg)
    def _():
        for d in range(mine):
            out_ref[0, pl.ds(d, tiles, stride=mine), :] = stage_ref[seg, d]

    @pl.when(half != seg)
    def _():
        for d in range(mine):
            out_ref[0, pl.ds(d, tiles, stride=mine), :] = arrived_ref[d]


def merge(share, stage, arrived, gathered):
    mine, tiles, _ = arrived.shape
    vmem = pl.BlockSpec(memory_space=pltpu.VMEM)
    return pl.pallas_call(
        functools.partial(merge_kernel, share),
        out_shape=(
            jax.ShapeDtypeStruct((2, tiles * mine, LANES), jnp.float32),
            jax.ShapeDtypeStruct((1, 1), jnp.float32),
        ),
        grid=(2,),
        in_specs=[vmem, vmem, vmem],
        out_specs=(
            pl.BlockSpec((1, tiles * mine, LANES), lambda i: (i, 0, 0)),
            pl.BlockSpec((1, 1), lambda i: (0, 0)),
        ),
        compiler_params=pltpu.CompilerParams(vmem_limit_bytes=16 << 20),
    )(stage, arrived, gathered)


def on_device(groups, monomer_density, monomer_centers, dimer_pairs, basis_sizes, dimer_core, esp_map, repulsion):
    dims, flat = dimer_core.shape
    mine = dims // 2
    tiles = flat // LANES
    core = dimer_core.reshape(2, mine, tiles, LANES).transpose(0, 2, 1, 3).reshape(2, tiles * mine, LANES)
    stage, arrived, gathered = solve(
        groups, monomer_density, monomer_centers, dimer_pairs, basis_sizes.reshape(1, -1), core, esp_map,
        repulsion.reshape(tiles, LANES),
    )
    section, total = merge(1.0 / dimer_pairs.shape[1], stage, arrived, gathered)
    section = section.reshape(2, tiles, mine, LANES).transpose(0, 2, 1, 3).reshape(1, dims, flat)
    return section, total[0, 0]


def solution(mesh):
    in_specs = (P("grp", None), P(), P(), P(), P("grp", None), P(), P())
    out_specs = (P("segment", "grp", None), P())
    return jax.shard_map(
        functools.partial(on_device, mesh.shape["grp"]), mesh=mesh, in_specs=in_specs, out_specs=out_specs, check_vma=False
    )
```

time: 64.6 us -> 55 us (0.85)
  Pallas kernels: 57.5 us -> 47.7 us
  local copies, waits for them, and re-layouts: 4.4 us -> 6.39 us
  between operations: 2.44 us -> 0.65 us
    pallas_call x3 -> x2, Pallas kernels: 57.5 us -> 47.7 us  [the longest x1 45.9 us: solve(): pl.pallas_call(functools.partial(solve_kernel, groups), out_shape=(KEEP((...]
    unnamed x1 -> x14, local copies, waits for them, and re-layouts: 3.22 us -> 6.39 us
    slice x1 -> x0, local copies, waits for them, and re-layouts: 1.17 us -> none  [on_device(): return (section, total[0, 0] / dimer_pairs.shape[1])]
where the time goes in v1:
time: 55 us; the launch traced here: 54.7 us
  Pallas kernels  47.7 us (87%)
  local copies, waits for them, and re-layouts  6.39 us (12%)
  between operations  0.65 us (1%)
    pallas_call x1, Pallas kernels, solve(): pl.pallas_call(functools.partial(solve_kernel, groups), out_shape=(KEEP((...  45.9 us
    unnamed x14, local copies, waits for them, and re-layouts  6.39 us
    pallas_call x1, Pallas kernels, merge(): pl.pallas_call(functools.partial(merge_kernel, share), out_shape=(jax.Sha...  1.8 us

profile of v1, /device:TPU:0, one launch (start us, length us, event | category | flops | bytes accessed | tf_op | source)
XLA Modules:
  0.0 54.7 jit_solution(14503315344820650112)
XLA Ops:
  0.6 0.0 copy-start
  0.6 1.7 %copy-done = f32[16,36864]{1,0:T(8,128)S(1)} copy-done((f32[16,36864]{1,0:T(8,128)S(1)}, f32[16,36864]{1,0:T(8,128)}, u32[]{:S(2)}) %copy-start) | copy-done | bytes 2359320
  2.3 0.0 copy-start.1
  2.3 0.9 %copy-done.1 = bf16[8,9216]{1,0:T(8,128)(2,1)S(1)} copy-done((bf16[8,9216]{1,0:T(8,128)(2,1)S(1)}, bf16[8,9216]{1,0:T(8,128)(2,1)}, u32[]{:S(2)}) %copy-start.1) | copy-done | bytes 147480
  3.2 0.0 copy-start.2
  3.2 0.9 %copy-done.2 = f32[36864]{0:T(1024)S(1)} copy-done((f32[36864]{0:T(1024)S(1)}, f32[36864]{0:T(1024)}, u32[]{:S(2)}) %copy-start.2) | copy-done | bytes 147480
  4.1 0.0 copy-start.3
  4.1 0.9 %copy-done.3 = f32[96,192]{1,0:T(8,128)S(1)} copy-done((f32[96,192]{1,0:T(8,128)S(1)}, f32[96,192]{1,0:T(8,128)}, u32[]{:S(2)}) %copy-start.3) | copy-done | bytes 73752
  5.0 0.0 copy-start.4
  5.0 0.7 %copy-done.4 = f32[3,128]{1,0:T(4,128)S(1)} copy-done((f32[3,128]{1,0:T(4,128)S(1)}, f32[3,128]{1,0:T(4,128)}, u32[]{:S(2)}) %copy-start.4) | copy-done | bytes 1560
  5.7 0.0 copy-start.5
  5.7 0.7 %copy-done.5 = s32[2,256]{1,0:T(2,128)S(1)} copy-done((s32[2,256]{1,0:T(2,128)S(1)}, s32[2,256]{1,0:T(2,128)}, u32[]{:S(2)}) %copy-start.5) | copy-done | bytes 2072
  6.4 0.0 copy-start.6
  6.4 0.7 %copy-done.6 = s32[128]{0:T(128)S(1)} copy-done((s32[128]{0:T(128)S(1)}, s32[128]{0:T(128)}, u32[]{:S(2)}) %copy-start.6) | copy-done | bytes 536
  7.0 45.9 %shard_map.86 = (f32[2,8,288,128]{3,2,1,0:T(8,128)S(1)}, f32[8,288,128]{2,1,0:T(8,128)S(1)}, f32[32,1,128]{2,1,0:T(1,128)S(1)}) custom-call(bf16[8,9216]{1,0:T(8,128)(2,1)S(1)} %copy-done.1, f32[3,128]{1,0:T(4,128)S(1)} %copy-done.4, s32[2,256]{1,0:T(2,128)S(1)} %copy-done.5, s32[1,128]{1,0:T(1,128)S(1)} %bitcast.15, f32[2,2304,128]{2,1,0:T(8,128)S(1)} %bitcast.13, ...), custom_call_target="tpu_custom_call" | custom-call | tf_op jit(solution)/shard_map/pallas_call | solution.py:345
  52.9 1.8 %shard_map.87 = (f32[2,2304,128]{2,1,0:T(8,128)}, f32[1,1]{1,0:T(1,128)}) custom-call(f32[2,8,288,128]{3,2,1,0:T(8,128)S(1)} %get-tuple-element.7.stage_ref, f32[8,288,128]{2,1,0:T(8,128)S(1)} %get-tuple-element.8.arrived_ref, f32[32,1,128]{2,1,0:T(1,128)S(1)} %get-tuple-element.9.gathered), custom_call_target="tpu_custom_call" | custom-call | tf_op jit(solution)/shard_map/pallas_call | solution.py:403
Async XLA Ops:
  0.6 1.7 %copy-start = (f32[16,36864]{1,0:T(8,128)S(1)}, f32[16,36864]{1,0:T(8,128)}, u32[]{:S(2)}) copy-start(f32[16,36864]{1,0:T(8,128)} %param.11) | copy-start | bytes 7077892
  2.3 0.9 %copy-start.1 = (bf16[8,9216]{1,0:T(8,128)(2,1)S(1)}, bf16[8,9216]{1,0:T(8,128)(2,1)}, u32[]{:S(2)}) copy-start(bf16[8,9216]{1,0:T(8,128)(2,1)} %density_ref.1) | copy-start | bytes 442372
  3.2 0.9 %copy-start.2 = (f32[36864]{0:T(1024)S(1)}, f32[36864]{0:T(1024)}, u32[]{:S(2)}) copy-start(f32[36864]{0:T(1024)} %param.13) | copy-start | bytes 442372
  4.1 0.9 %copy-start.3 = (f32[96,192]{1,0:T(8,128)S(1)}, f32[96,192]{1,0:T(8,128)}, u32[]{:S(2)}) copy-start(f32[96,192]{1,0:T(8,128)} %map_ref.1) | copy-start | bytes 221188
  5.0 0.7 %copy-start.4 = (f32[3,128]{1,0:T(4,128)S(1)}, f32[3,128]{1,0:T(4,128)}, u32[]{:S(2)}) copy-start(f32[3,128]{1,0:T(4,128)} %centers_ref.1) | copy-start | bytes 4612
  5.7 0.7 %copy-start.5 = (s32[2,256]{1,0:T(2,128)S(1)}, s32[2,256]{1,0:T(2,128)}, u32[]{:S(2)}) copy-start(s32[2,256]{1,0:T(2,128)} %pairs_ref.1) | copy-start | bytes 6148
  6.4 0.7 %copy-start.6 = (s32[128]{0:T(128)S(1)}, s32[128]{0:T(128)}, u32[]{:S(2)}) copy-start(s32[128]{0:T(128)} %param.10) | copy-start | bytes 1540

commit v2 on v1

--- a/solution.py
+++ b/solution.py
@@ -10,7 +10,7 @@
 PURIFY = 8
 epsilon = 1e-06
 LANES = 128
-SPLITS = 2
+SPLITS = 3
 KEEP = pltpu.VMEM
 MESH = pl.DeviceIdType.MESH
 FIRST_PLAN = ((1, 1),) * PURIFY
@@ -100,10 +100,11 @@
 
 
 def solve_kernel(
-    groups, density_ref, centers_ref, pairs_ref, sizes_ref, core_ref, map_ref, rep_ref,
-    stage_ref, arrived_ref, gathered,
-    blocks, given, field_ref, core_buf, low, high, fbuf, fock, iterate, energy_ref,
+    groups, density_ref, centers_hbm, pairs_hbm, sizes_hbm, core_ref, map_hbm, rep_hbm,
+    stage_ref, arrived_ref, total_ref,
+    gathered, blocks, given, field_ref, core_buf, low, high, fbuf, fock, iterate, energy_ref,
     send_sem, recv_sem, own_sem, part_send, part_recv, sum_send, sum_recv, section_send, section_recv, core_sem,
+    centers_ref, pairs_ref, sizes_ref, map_ref, rep_ref, small_sem,
 ):
     me = lax.axis_index("grp")
     seg = lax.axis_index("segment")
@@ -127,8 +128,9 @@
         return other // groups, lax.rem(other, groups)
 
     barrier = pltpu.get_barrier_semaphore()
-    for offset in range(1, devices):
-        pl.semaphore_signal(barrier, inc=1, device_id=place_of(offset), device_id_type=MESH)
+    for bit in sorted(orders[0]):
+        pl.semaphore_signal(barrier, inc=1, device_id=(seg, me ^ bit), device_id_type=MESH)
+    pl.semaphore_signal(barrier, inc=1, device_id=(1 - seg, me), device_id_type=MESH)
     own = []
     for f in range(flows):
         start = pl.multiple_of(seg * half + f * columns, LANES)
@@ -138,7 +140,14 @@
         own.append(copy)
     fetch = pltpu.make_async_copy(core_ref.at[seg], core_buf, core_sem)
     fetch.start()
-    pl.semaphore_wait(barrier, devices - 1)
+    small = []
+    for i, (source, target) in enumerate((
+        (centers_hbm, centers_ref), (pairs_hbm, pairs_ref), (sizes_hbm, sizes_ref), (map_hbm, map_ref), (rep_hbm, rep_ref),
+    )):
+        copy = pltpu.make_async_copy(source, target, small_sem.at[i])
+        copy.start()
+        small.append(copy)
+    pl.semaphore_wait(barrier, stages + 1)
 
     def exchange(f, k):
         count = 1 << k
@@ -154,6 +163,9 @@
     for f in range(flows):
         own[f].wait()
         exchange(f, 0).start()
+
+    for copy in small:
+        copy.wait()
 
     place = iota((dims, 1), 0)
     positions = me * dims + jnp.where(place < mine, seg * mine + place, (1 - seg) * mine + place - mine)
@@ -236,16 +248,21 @@
             out.append(jnp.where(at.astype(jnp.float32) < limit, 1.0, 0.0))
         return out, first + second
 
-    def total(value):
-        return jnp.sum(jnp.sum(value, axis=0, keepdims=True), axis=1, keepdims=True)
-
-    def begin(matrix, d):
-        (live_row, live_column), count = live(d)
-        masked = matrix * (live_column * live_row)
-        chemical = total(jnp.where(eye, masked, 0.0)) / count
-        shifted = masked - jnp.where(eye, chemical * live_row, 0.0)
-        radius = jnp.max(jnp.sum(jnp.abs(shifted), axis=0, keepdims=True), axis=1, keepdims=True)
-        iterate[d] = shifted * (-1.0 / (radius + epsilon))
+    def begin_all(matrices):
+        masks = [live(d) for d in range(mine)]
+        for d in range(mine):
+            (live_row, live_column), count = masks[d]
+            iterate[d] = matrices[d]() * (live_column * live_row)
+        traces = [jnp.sum(jnp.where(eye, iterate[d], 0.0), axis=0, keepdims=True) for d in range(mine)]
+        levels = [jnp.sum(t, axis=1, keepdims=True) / masks[d][1] for d, t in enumerate(traces)]
+        sums = []
+        for d in range(mine):
+            shifted = iterate[d] - jnp.where(eye, levels[d] * masks[d][0][0], 0.0)
+            iterate[d] = shifted
+            sums.append(jnp.sum(jnp.abs(shifted), axis=0, keepdims=True))
+        scales = [-1.0 / (jnp.max(t, axis=1, keepdims=True) + epsilon) for t in sums]
+        for d in range(mine):
+            iterate[d] = iterate[d] * scales[d]
 
     def step(passes):
         first, second = passes
@@ -281,12 +298,12 @@
             device_id=(1 - seg, me), device_id_type=MESH,
         )
 
-    for d in range(mine):
-        field = load_field(field_ref, fbuf.at[d], d, width)
-        field = 0.5 * (field + field.T)
-        value = fock[d] + product(mapping_t, product(field, mapping, 3), 3)
-        fock[d] = value
-        begin(value, d)
+    fields = [load_field(field_ref, fbuf.at[d], d, width) for d in range(mine)]
+    fields = [0.5 * (field + field.T) for field in fields]
+    lefts = [product(field, mapping, 3) for field in fields]
+    for d in range(mine):
+        fock[d] = fock[d] + product(mapping_t, lefts[d], 3)
+    begin_all([lambda d=d: fock[d] for d in range(mine)])
     for d in range(mine):
         store_square(stage_ref.at[0, d], fock[d], low.at[d], high.at[d], full)
 
@@ -296,25 +313,23 @@
             swap(0, d).start()
 
     run(FIRST_PLAN)
-    for d in range(mine):
+    def rebuilt(d):
         density, count = finish(d)
         occupied = jnp.sum(jnp.where(eye, density, 0.0), axis=1, keepdims=True)
         coulomb = jnp.sum(symmetric * occupied, axis=0, keepdims=True)
         change = jnp.where(eye, coulomb, 0.0) - 0.5 * symmetric * density
         core_fock = fock[d]
-        begin(core_fock + change, d)
         fock[d] = 2.0 * core_fock + change
+        return core_fock + change
+
+    begin_all([functools.partial(rebuilt, d) for d in range(mine)])
     run(LAST_PLAN)
-    energy = jnp.zeros((1, 1), jnp.float32)
+    partials = jnp.zeros((1, full), jnp.float32)
     for d in range(mine):
         density, count = finish(d)
-        energy = energy + 0.5 * total(density * fock[d]) / count
-        store_square(stage_ref.at[1, d], density, low.at[d], high.at[d], full)
-
-        @pl.when(seg == 0)
-        def _():
-            swap(1, d).start()
-
+        iterate[d] = density
+        partials = partials + jnp.sum(density * fock[d], axis=0, keepdims=True) * (0.5 / count)
+    energy = jnp.sum(partials, axis=1, keepdims=True)
     energy_ref[...] = jnp.broadcast_to(energy, energy_ref.shape)
     gathered[index] = energy_ref[...]
     copies = []
@@ -325,8 +340,16 @@
         )
         copy.start()
         copies.append(copy)
+    for d in range(mine):
+        store_square(stage_ref.at[1, d], iterate[d], low.at[d], high.at[d], full)
+
+        @pl.when(seg == 0)
+        def _():
+            swap(1, d).start()
+
     for copy in copies:
         copy.wait()
+    total_ref[...] = jnp.sum(gathered[...], axis=0)
     for d in range(mine):
         swap(1 - seg, d).wait()
 
@@ -347,11 +370,12 @@
         out_shape=(
             KEEP((2, mine, tiles, LANES), jnp.float32),
             KEEP((mine, tiles, LANES), jnp.float32),
-            KEEP((devices, 1, LANES), jnp.float32),
+            KEEP((1, LANES), jnp.float32),
         ),
-        in_specs=[anywhere, vmem, vmem, vmem, anywhere, vmem, vmem],
+        in_specs=[anywhere] * 7,
         out_specs=(vmem, vmem, vmem),
         scratch_shapes=[
+            pltpu.VMEM((devices, 1, LANES), jnp.float32),
             pltpu.VMEM((flows, groups, rows, half // flows), jnp.bfloat16),
             pltpu.VMEM((half // LANES, mine, LANES), jnp.float32),
             pltpu.VMEM((total // LANES, mine, LANES), jnp.float32),
@@ -372,19 +396,21 @@
             pltpu.SemaphoreType.DMA((mine,)),
             pltpu.SemaphoreType.DMA((mine,)),
             pltpu.SemaphoreType.DMA,
+            *[pltpu.VMEM(small.shape, small.dtype) for small in (centers, pairs, sizes, mapping, repulsion)],
+            pltpu.SemaphoreType.DMA((5,)),
         ],
-        compiler_params=pltpu.CompilerParams(collective_id=0, has_side_effects=True, vmem_limit_bytes=40 << 20),
+        compiler_params=pltpu.CompilerParams(collective_id=0, has_side_effects=True),
     )(density, centers, pairs, sizes, core, mapping, repulsion)
 
 
-def merge_kernel(share, stage_ref, arrived_ref, gathered, out_ref, total_ref):
+def merge_kernel(share, stage_ref, arrived_ref, sum_ref, out_ref, total_ref):
     seg = lax.axis_index("segment")
     half = pl.program_id(0)
     mine, tiles, _ = arrived_ref.shape
 
     @pl.when(half == 0)
     def _():
-        total_ref[...] = jnp.sum(gathered[...], axis=0)[:, :1] * share
+        total_ref[...] = sum_ref[:, :1] * share
 
     @pl.when(half == seg)
     def _():

time: 55 us -> 45.7 us (0.83)
  local copies, waits for them, and re-layouts: 6.39 us -> 0 us
  Pallas kernels: 47.7 us -> 44.9 us
    unnamed x14 -> x0, local copies, waits for them, and re-layouts: 6.39 us -> none
    pallas_call x1, Pallas kernels: 45.9 us -> 43.1 us  [solve(): pl.pallas_call(functools.partial(solve_kernel, groups), out_shape=(KEEP((...]
where the time goes in v2:
time: 45.7 us; the launch traced here: 45.6 us
  Pallas kernels  44.9 us (98%)
  between operations  0.64 us (1%)
    pallas_call x1, Pallas kernels, solve(): pl.pallas_call(functools.partial(solve_kernel, groups), out_shape=(KEEP((...  43.1 us
    pallas_call x1, Pallas kernels, merge(): pl.pallas_call(functools.partial(merge_kernel, share), out_shape=(jax.Sha...  1.78 us

profile of v2, /device:TPU:0, one launch (start us, length us, event | category | flops | bytes accessed | tf_op | source)
XLA Modules:
  0.0 45.6 jit_solution(8709345251638135148)
XLA Ops:
  0.6 43.1 %shard_map.86 = (f32[2,8,288,128]{3,2,1,0:T(8,128)S(1)}, f32[8,288,128]{2,1,0:T(8,128)S(1)}, f32[1,128]{1,0:T(1,128)S(1)}) custom-call(bf16[8,9216]{1,0:T(8,128)(2,1)} %density_ref.1, f32[3,128]{1,0:T(4,128)} %centers_hbm.1, s32[2,256]{1,0:T(2,128)} %pairs_hbm.1, s32[1,128]{1,0:T(1,128)} %bitcast.15, f32[2,2304,128]{2,1,0:T(8,128)} %bitcast.13, ...), custom_call_target="tpu_custom_call" | custom-call | tf_op jit(solution)/shard_map/pallas_call | solution.py:368
  43.8 1.8 %shard_map.87 = (f32[2,2304,128]{2,1,0:T(8,128)}, f32[1,1]{1,0:T(1,128)}) custom-call(f32[2,8,288,128]{3,2,1,0:T(8,128)S(1)} %get-tuple-element.7.stage_ref, f32[8,288,128]{2,1,0:T(8,128)S(1)} %get-tuple-element.8.arrived_ref, f32[1,128]{1,0:T(1,128)S(1)} %get-tuple-element.9.sum_ref), custom_call_target="tpu_custom_call" | custom-call | tf_op jit(solution)/shard_map/pallas_call | solution.py:429

commit v3 on v2

--- a/solution.py
+++ b/solution.py
@@ -14,7 +14,7 @@
 KEEP = pltpu.VMEM
 MESH = pl.DeviceIdType.MESH
 FIRST_PLAN = ((1, 1),) * PURIFY
-LAST_PLAN = ((1, 1),) * (PURIFY - 3) + ((3, 3),) * 3
+LAST_PLAN = ((1, 1),) * (PURIFY - 2) + ((3, 3),) * 2
 
 
 def flow_orders(groups):

time: 45.7 us -> 44.9 us (0.982)
  Pallas kernels: 44.9 us -> 44.1 us
    pallas_call x1, Pallas kernels: 43.1 us -> 42.3 us  [solve(): pl.pallas_call(functools.partial(solve_kernel, groups), out_shape=(KEEP((...]
where the time goes in v3:
time: 44.9 us; the launch traced here: 44.7 us
  Pallas kernels  44.1 us (98%)
  between operations  0.64 us (1%)
    pallas_call x1, Pallas kernels, solve(): pl.pallas_call(functools.partial(solve_kernel, groups), out_shape=(KEEP((...  42.3 us
    pallas_call x1, Pallas kernels, merge(): pl.pallas_call(functools.partial(merge_kernel, share), out_shape=(jax.Sha...  1.78 us

profile of v3, /device:TPU:0, one launch (start us, length us, event | category | flops | bytes accessed | tf_op | source)
XLA Modules:
  0.0 44.7 jit_solution(6862005718134853414)
XLA Ops:
  0.6 42.3 %shard_map.86 = (f32[2,8,288,128]{3,2,1,0:T(8,128)S(1)}, f32[8,288,128]{2,1,0:T(8,128)S(1)}, f32[1,128]{1,0:T(1,128)S(1)}) custom-call(bf16[8,9216]{1,0:T(8,128)(2,1)} %density_ref.1, f32[3,128]{1,0:T(4,128)} %centers_hbm.1, s32[2,256]{1,0:T(2,128)} %pairs_hbm.1, s32[1,128]{1,0:T(1,128)} %bitcast.15, f32[2,2304,128]{2,1,0:T(8,128)} %bitcast.13, ...), custom_call_target="tpu_custom_call" | custom-call | tf_op jit(solution)/shard_map/pallas_call | solution.py:368
  43.0 1.8 %shard_map.87 = (f32[2,2304,128]{2,1,0:T(8,128)}, f32[1,1]{1,0:T(1,128)}) custom-call(f32[2,8,288,128]{3,2,1,0:T(8,128)S(1)} %get-tuple-element.7.stage_ref, f32[8,288,128]{2,1,0:T(8,128)S(1)} %get-tuple-element.8.arrived_ref, f32[1,128]{1,0:T(1,128)S(1)} %get-tuple-element.9.sum_ref), custom_call_target="tpu_custom_call" | custom-call | tf_op jit(solution)/shard_map/pallas_call | solution.py:429
